TPU v7x, 32 devices: a whole 2x2x4 slice. The times are simulated.
32 devices in a mesh: tm: 8 (over y, x, core), mp: 4 (over z).
Axes of the slice: x: 2, y: 2, z: 4, core: 2. Of those that a mesh axis runs over, the one named last changes fastest.
Arguments:
- frames: bfloat16 [4096, 1024], P(('tm', 'mp')), may hold values from -6 to 6
- block_ids: int32 [4096], replicated, may hold values from 0 to 203, never falling along the last dimension, each value on 1 to 40 neighbouring positions
- valid_counts: int32 [8], replicated, may hold values from 1 to 512, as said below
- norm_attn: float32 [1024], replicated, may hold values from 0.25 to 1.75
- w_qkv: bfloat16 [1024, 3072], replicated, may hold values from -1 to 1
- w_attn_out: bfloat16 [1024, 1024], replicated, may hold values from -0.1875 to 0.1875
- norm_conv: float32 [1024], replicated, may hold values from 0.25 to 1.75
- w_point_in: bfloat16 [1024, 2048], replicated, may hold values from -0.1875 to 0.1875
- w_depth: bfloat16 [31, 1024], replicated, may hold values from -1 to 1
- w_point_out: bfloat16 [1024, 1024], replicated, may hold values from -0.1875 to 0.1875
- w_adapter: bfloat16 [1024, 8192], P('tm', 'mp'), may hold values from -1 to 1
- llm_gain: float32 [8192], replicated, may hold values from 0.25 to 1.75
- w_query: bfloat16 [8192, 8192], P('tm', 'mp'), may hold values from -1 to 1
- w_key: bfloat16 [8192, 1024], P('tm', 'mp'), may hold values from -1 to 1
- w_value: bfloat16 [8192, 1024], P('tm', 'mp'), may hold values from -0.0625 to 0.0625
Outputs:
- conf_out: bfloat16 [4096, 1024], P(('tm', 'mp'))
- attended: bfloat16 [1024, 8192], P('tm', 'mp')
Inputs may be any that keep to these rules, and one draw needn't show every extreme that they name: `block_ids`: block numbers never fall along the recording, and one block holds 1 to 40 frames. Every time shard but the last holds 512 real frames; the frames after the first valid_counts[t] of time shard t are padding.
All inputs are finite; a program needn't handle non-finite values.
Results may differ from a plain program's by a relative error of at most 0.014.
Values may be sent and summed in bfloat16 or wider, within the bound.
No kernel may reach another device: no remote copies, remote signals or barrier semaphores. Data moves between devices by JAX's collectives and lax.ppermute only.
A program may use at most 192 MiB of HBM per device.

v0:
```python
import math
import jax
import jax.numpy as jnp
from jax import lax
from jax.sharding import PartitionSpec as P

CH = 16
HDIM = 128
eps_conf = 1e-05
eps_llm = 1e-06
rope_base = 1000000.0
masked_score = -1e30


def passed_along(value, axis, by):
    length = lax.axis_size(axis)
    pairs = [(i, i + by) for i in range(length) if 0 <= i + by < length]
    return lax.ppermute(value, axis, pairs)


def shard_count(index, valid_counts, shard_len):
    shard = index // shard_len
    table = jnp.arange(valid_counts.shape[0], dtype=jnp.int32)
    hit = shard[:, None] == table[None, :]
    count = jnp.sum(jnp.where(hit, valid_counts[None, :], 0), axis=1)
    return (index - shard * shard_len, count)


def layer_norm(field, gain):
    center = field - jnp.mean(field, axis=-1, keepdims=True)
    spread = jnp.mean(center * center, axis=-1, keepdims=True)
    return center * lax.rsqrt(spread + eps_conf) * gain


def rotary(field, positions):
    half = field.shape[-1] // 2
    freq = rope_base ** (-(jnp.arange(half, dtype=jnp.float32) * 2.0) / field.shape[-1])
    angle = positions.astype(jnp.float32)[:, None] * freq[None, :]
    cosine = jnp.concatenate([jnp.cos(angle), jnp.cos(angle)], axis=-1)[:, None, :]
    sine = jnp.concatenate([jnp.sin(angle), jnp.sin(angle)], axis=-1)[:, None, :]
    turned = jnp.concatenate([-field[..., half:], field[..., :half]], axis=-1)
    return field * cosine + turned * sine


def on_device(
    frames,
    block_ids,
    valid_counts,
    norm_attn,
    w_qkv,
    w_attn_out,
    norm_conv,
    w_point_in,
    w_depth,
    w_point_out,
    w_adapter,
    llm_gain,
    w_query,
    w_key,
    w_value,
):
    mp_count = lax.axis_size("mp")
    frame_rows, width = frames.shape
    heads = CH
    head_size = width // heads
    shard_frames = frame_rows * mp_count
    time_place = lax.axis_index("tm")
    model_place = lax.axis_index("mp")
    first = (time_place * mp_count + model_place) * frame_rows
    inputs = frames.astype(jnp.float32)
    own_index = first + jnp.arange(frame_rows, dtype=jnp.int32)
    own_place, own_count = shard_count(own_index, valid_counts, shard_frames)
    frame_real = own_place < own_count
    normed = layer_norm(inputs, norm_attn).astype(jnp.bfloat16)
    projected = jnp.dot(normed, w_qkv, preferred_element_type=jnp.float32).astype(jnp.bfloat16)
    queries = projected[:, :width]
    own_keys = projected[:, width : 2 * width]
    own_values = projected[:, 2 * width :]
    prior_keys, prior_values = passed_along((own_keys, own_values), ("tm", "mp"), 1)
    keys = jnp.concatenate([prior_keys, own_keys], axis=0).reshape(2 * frame_rows, heads, head_size)
    values = jnp.concatenate([prior_values, own_values], axis=0).reshape(
        2 * frame_rows, heads, head_size
    )
    key_index = first - frame_rows + jnp.arange(2 * frame_rows, dtype=jnp.int32)
    key_place, key_count = shard_count(key_index, valid_counts, shard_frames)
    key_real = key_place < key_count
    prior_ids = lax.dynamic_slice_in_dim(
        block_ids, jnp.maximum(first - frame_rows, 0), frame_rows, 0
    )
    query_ids = lax.dynamic_slice_in_dim(block_ids, first, frame_rows, 0)
    key_ids = jnp.concatenate([prior_ids, query_ids], axis=0)
    same = key_index[None, :] == own_index[:, None]
    visible = (
        (key_index[None, :] <= own_index[:, None])
        & (key_ids[None, :] >= query_ids[:, None] - 2)
        & (key_real[None, :] | same)
    )
    query_heads = queries.reshape(frame_rows, heads, head_size)
    scores = jnp.einsum(
        "qhd,khd->hqk", query_heads, keys, preferred_element_type=jnp.float32
    ) / jnp.sqrt(jnp.float32(head_size))
    scores = jnp.where(visible[None], scores, masked_score)
    top = jnp.max(scores, axis=-1, keepdims=True)
    weights = jnp.where(visible[None], jnp.exp(scores - top), 0.0)
    total = jnp.sum(weights, axis=-1)
    summed = jnp.einsum(
        "hqk,khd->qhd", weights.astype(jnp.bfloat16), values, preferred_element_type=jnp.float32
    )
    conf_context = (
        (summed / jnp.transpose(total)[:, :, None]).reshape(frame_rows, width).astype(jnp.bfloat16)
    )
    mid = inputs + jnp.dot(conf_context, w_attn_out, preferred_element_type=jnp.float32)
    conv_in = layer_norm(mid, norm_conv).astype(jnp.bfloat16)
    both = jnp.dot(conv_in, w_point_in, preferred_element_type=jnp.float32)
    glu = both[:, :width] * jax.nn.sigmoid(both[:, width:])
    glu = jnp.where(frame_real[:, None], glu, 0.0).astype(jnp.bfloat16)
    taps = w_depth.shape[0]
    rim = passed_along(glu[frame_rows - (taps - 1) :], ("tm", "mp"), 1)
    padded = jnp.concatenate([rim, glu], axis=0).astype(jnp.float32)
    kernel = w_depth.astype(jnp.float32)
    depth = jnp.zeros((frame_rows, width), jnp.float32)
    for tap in range(taps):
        depth = depth + kernel[tap][None, :] * padded[taps - 1 - tap : taps - 1 - tap + frame_rows]
    activated = jax.nn.silu(depth).astype(jnp.bfloat16)
    final = mid + jnp.dot(activated, w_point_out, preferred_element_type=jnp.float32)
    conf_out = jnp.where(frame_real[:, None], final, 0.0).astype(jnp.bfloat16)
    pooled = (
        jnp.sum(conf_out.astype(jnp.float32).reshape(frame_rows // 4, 4, width), axis=1) * 0.25
    ).astype(jnp.bfloat16)
    shard_pooled = lax.all_gather(pooled, "mp", axis=0, tiled=True)
    shard_tokens = shard_pooled.shape[0]
    adapter_part = lax.all_gather(w_adapter, "tm", axis=0, tiled=True)
    adapter_full = lax.all_gather(adapter_part, "mp", axis=1, tiled=True)
    adapted = jnp.dot(shard_pooled, adapter_full, preferred_element_type=jnp.float32)
    llm_in = (
        adapted
        * lax.rsqrt(jnp.mean(adapted * adapted, axis=-1, keepdims=True) + eps_llm)
        * llm_gain
    ).astype(jnp.bfloat16)
    query_cols = w_query.shape[1]
    key_cols = w_key.shape[1]
    raw_query = jnp.dot(
        llm_in,
        lax.all_gather(w_query, "tm", axis=0, tiled=True),
        preferred_element_type=jnp.float32,
    )
    raw_keys = jnp.dot(
        llm_in, lax.all_gather(w_key, "tm", axis=0, tiled=True), preferred_element_type=jnp.float32
    )
    raw_values = jnp.dot(
        llm_in,
        lax.all_gather(w_value, "tm", axis=0, tiled=True),
        preferred_element_type=jnp.float32,
    )
    llm_size = HDIM
    query_heads_dev = query_cols // llm_size
    kv_heads = key_cols // llm_size
    group = query_heads_dev // kv_heads
    token_index = time_place * shard_tokens + jnp.arange(shard_tokens, dtype=jnp.int32)
    llm_query = rotary(
        raw_query.reshape(shard_tokens, query_heads_dev, llm_size), token_index
    ).astype(jnp.bfloat16)
    llm_query = llm_query.reshape(shard_tokens, kv_heads, group, llm_size)
    llm_keys = (
        rotary(raw_keys.reshape(shard_tokens, kv_heads, llm_size), token_index)
        .astype(jnp.bfloat16)
        .reshape(shard_tokens, key_cols)
    )
    llm_values = raw_values.astype(jnp.bfloat16)
    score_scale = 1.0 / jnp.sqrt(jnp.float32(llm_size))
    start_state = (
        jnp.full((kv_heads, group, shard_tokens), masked_score, jnp.float32),
        jnp.zeros((kv_heads, group, shard_tokens), jnp.float32),
        jnp.zeros((kv_heads, group, shard_tokens, llm_size), jnp.float32),
    )
    key_piece = lax.all_gather(llm_keys, "tm", axis=0, tiled=True)
    value_piece = lax.all_gather(llm_values, "tm", axis=0, tiled=True)
    piece_rows = key_piece.shape[0]
    step_rows = math.gcd(piece_rows, 512)

    def one_step(block, state):
        best, total_weight, accum = state
        key_block = lax.dynamic_slice_in_dim(key_piece, block * step_rows, step_rows, 0).reshape(
            step_rows, kv_heads, llm_size
        )
        value_block = lax.dynamic_slice_in_dim(
            value_piece, block * step_rows, step_rows, 0
        ).reshape(step_rows, kv_heads, llm_size)
        block_index = block * step_rows + jnp.arange(step_rows, dtype=jnp.int32)
        block_place, block_count = shard_count(block_index, valid_counts, shard_tokens)
        block_real = block_place * 4 < block_count
        matches = block_index[None, :] == token_index[:, None]
        seen = (block_index[None, :] <= token_index[:, None]) & (block_real[None, :] | matches)
        block_scores = (
            jnp.einsum("qhgd,khd->hgqk", llm_query, key_block, preferred_element_type=jnp.float32)
            * score_scale
        )
        block_scores = jnp.where(seen[None, None], block_scores, masked_score)
        new_best = jnp.maximum(best, jnp.max(block_scores, axis=-1))
        block_weights = jnp.where(
            seen[None, None], jnp.exp(block_scores - new_best[..., None]), 0.0
        )
        fade = jnp.exp(best - new_best)
        total_weight = total_weight * fade + jnp.sum(block_weights, axis=-1)
        accum = accum * fade[..., None] + jnp.einsum(
            "hgqk,khd->hgqd",
            block_weights.astype(jnp.bfloat16),
            value_block,
            preferred_element_type=jnp.float32,
        )
        return (new_best, total_weight, accum)

    best, total_weight, accum = lax.fori_loop(0, piece_rows // step_rows, one_step, start_state)
    result = accum / total_weight[..., None]
    attended = (
        jnp.transpose(result, (2, 0, 1, 3)).reshape(shard_tokens, query_cols).astype(jnp.bfloat16)
    )
    return (conf_out, attended)


def solution(mesh):
    placed = (
        P(("tm", "mp"), None),
        P(),
        P(),
        P(),
        P(),
        P(),
        P(),
        P(),
        P(),
        P(),
        P("tm", "mp"),
        P(),
        P("tm", "mp"),
        P("tm", "mp"),
        P("tm", "mp"),
    )
    return jax.shard_map(
        on_device,
        mesh=mesh,
        in_specs=placed,
        out_specs=(P(("tm", "mp"), None), P("tm", "mp")),
        check_vma=False,
    )
```

profile of v0, /device:TPU:0, one launch (start us, length us, event | category | flops | bytes accessed | tf_op | source)
XLA Modules:
  0.0 644.8 jit_solution(2328061743884182033)
XLA Ops:
  7.2 0.7 all-gather.6.cloned.1.call-update
  8.0 41.4 %all-gather.6.cloned.1.call-done = bf16[1024,2048]{1,0:T(8,128)(2,1)} async-done(((bf16[128,2048]{1,0:T(8,128)(2,1)}), bf16[1024,2048]{1,0:T(8,128)(2,1)}) %all-gather.6.cloned.1.call-update) | async-done | bytes 4194320 | tf_op jit(solution)/shard_map/all_gather | solution.py:132
  49.4 0.7 all-gather.10.cloned.1.call-update
  50.2 0.5 all-gather.14.cloned.1.call-update
  50.7 0.5 all-gather.12.cloned.1.call-update
  51.4 0.2 fusion.32
  51.7 3.9 convolution_convert_fusion
  55.6 0.8 fusion.92
  56.3 3.4 collective-permute-start.1
  59.7 4.1 collective-permute-start
  63.9 0.9 broadcast_add_fusion
  64.9 0.7 or_and_fusion.1
  65.6 0.7 fusion.94
  66.2 0.7 fusion.93
  66.9 0.3 multiply_cosine_fusion
  67.3 0.8 copy.53
  68.2 0.6 subtract_compare_fusion.1
  68.7 0.6 collective-permute-done.1
  69.6 10.4 %collective-permute-done = bf16[128,1024]{1,0:T(8,128)(2,1)} collective-permute-done((bf16[128,1024]{1,0:T(8,128)(2,1)}, bf16[128,1024]{1,0:T(8,128)(2,1)}, u32[]{:S(2)}, u32[]{:S(2)}) %collective-permute-start) | collective-permute-done | bytes 262176 | tf_op jit(solution)/shard_map/ppermute | solution.py:18
  80.0 1.1 pad_maximum_fusion
  81.1 1.0 copy.52
  82.1 2.0 fusion.95
  84.1 1.8 fusion.97
  86.0 3.9 fusion.22
  89.9 0.5 fusion.96
  90.4 0.2 multiply_reduce_fusion.1
  91.0 3.1 fusion.72
  94.3 13.2 %collective-permute-start.2 = (bf16[30,1024]{1,0:T(8,128)(2,1)S(1)}, bf16[30,1024]{1,0:T(8,128)(2,1)S(1)}, u32[]{:S(2)}, u32[]{:S(2)}) collective-permute-start(bf16[30,1024]{1,0:T(8,128)(2,1)S(1)} %slice.294), channel_id=1, source_target_pairs={{0,1},{1,2},{2,3},{3,4},{4,5},{5,6},{6,7},{7,8},{8,9},{9,10},{10,1... | collective-permute-start | bytes 184328 | tf_op jit(solution)/shard_map/ppermute | solution.py:18
  107.6 3.0 collective-permute-done.2
  111.1 2.5 fusion.23
  113.8 0.3 reduce_sum.120
  114.1 36.5 %all_gather.24 = bf16[128,1024]{1,0:T(8,128)(2,1)S(1)} all-gather(bf16[32,1024]{1,0:T(8,128)(2,1)S(1)} %multiply_convert_fusion.5), channel_id=1, replica_groups=mesh['tm'=8,'mp'=4] {'mp'}, dimensions={0}, use_global_device_ids=true | all-gather | bytes 327680 | tf_op jit(solution)/shard_map/all_gather | solution.py:130
  150.6 200.2 %all-gather.8.cloned.1.call-done = bf16[1024,8192]{1,0:T(8,128)(2,1)} async-done(((bf16[1024,2048]{1,0:T(8,128)(2,1)}), bf16[1024,8192]{1,0:T(8,128)(2,1)}) %all-gather.8.cloned.1.call-update) | async-done | bytes 16777232 | tf_op jit(solution)/shard_map/all_gather | solution.py:133
  350.8 8.2 %multiply_reduce_fusion = (f32[128]{0:T(128)S(1)}, f32[128,8192]{1,0:T(8,128)S(1)}) fusion(bf16[128,1024]{1,0:T(8,128)(2,1)S(1)} %all_gather.24, bf16[1024,8192]{1,0:T(8,128)(2,1)} %all-gather.8.cloned.1.call-done), kind=kOutput, calls=%fused_computation.35 | convolution fusion | flops 2149580800 | bytes 21234176 | tf_op jit(solution)/shard_map/dot_general | solution.py:134
  359.0 0.5 multiply_convert_fusion
  359.5 27.4 %all-gather.10.cloned.1.call-done = bf16[8192,256]{1,0:T(8,128)(2,1)} async-done(((bf16[1024,256]{1,0:T(8,128)(2,1)}), bf16[8192,256]{1,0:T(8,128)(2,1)}) %all-gather.10.cloned.1.call-update) | async-done | bytes 4194320 | tf_op jit(solution)/shard_map/all_gather | solution.py:148
  386.9 2.9 fusion.98
  389.9 0.2 slice_negate_fusion.2
  390.1 0.2 maximum_multiply_fusion.1
  390.4 12.2 %all_gather.28 = bf16[1024,256]{1,0:T(8,128)(2,1)} all-gather(bf16[128,256]{1,0:T(8,128)(2,1)S(1)} %fusion.82), channel_id=1, replica_groups=mesh['tm'=8,'mp'=4] {'tm'}, dimensions={0}, use_global_device_ids=true | all-gather | bytes 589824 | tf_op jit(solution)/shard_map/all_gather | solution.py:176
  402.6 23.5 %all-gather.14.cloned.1.call-done = bf16[8192,256]{1,0:T(8,128)(2,1)} async-done(((bf16[1024,256]{1,0:T(8,128)(2,1)}), bf16[8192,256]{1,0:T(8,128)(2,1)}) %all-gather.14.cloned.1.call-update) | async-done | bytes 4194320 | tf_op jit(solution)/shard_map/all_gather | solution.py:152
  426.1 2.9 convolution_convert_fusion.1
  429.0 10.8 %all_gather.31 = bf16[1024,256]{1,0:T(8,128)(2,1)} all-gather(bf16[128,256]{1,0:T(8,128)(2,1)S(1)} %convolution_convert_fusion.1), channel_id=1, replica_groups=mesh['tm'=8,'mp'=4] {'tm'}, dimensions={0}, use_global_device_ids=true | all-gather | bytes 589824 | tf_op jit(solution)/shard_map/all_gather | solution.py:177
  439.8 148.9 %all-gather.12.cloned.1.call-done = bf16[8192,2048]{1,0:T(8,128)(2,1)} async-done(((bf16[1024,2048]{1,0:T(8,128)(2,1)}), bf16[8192,2048]{1,0:T(8,128)(2,1)}) %all-gather.12.cloned.1.call-update) | async-done | bytes 33554448 | tf_op jit(solution)/shard_map/all_gather | solution.py:144
  588.7 12.9 %fusion.99 = f32[128,2048]{1,0:T(8,128)S(1)} fusion(bf16[128,8192]{1,0:T(8,128)(2,1)S(1)} %multiply_convert_fusion, bf16[8192,2048]{1,0:T(8,128)(2,1)} %all-gather.12.cloned.1.call-done), kind=kOutput, calls=%fused_computation.199 | convolution fusion | flops 4294967296 | bytes 36700160 | tf_op jit(solution)/shard_map/dot_general | solution.py:142
  601.6 0.3 copy.56
  601.9 1.1 slice_negate_fusion
  603.0 2.4 copy.57
  605.4 2.4 copy.58
  608.0 2.2 fusion.25
  610.2 25.0 %while.20 = (s32[]{:T(128)}, f32[2,8,128]{2,1,0:T(8,128)S(1)}, f32[2,8,128]{2,1,0:T(8,128)S(1)}, f32[2,8,128,128]{3,2,1,0:T(8,128)}, s32[8]{0:T(128)S(1)}, /*ind...) while((s32[]{:T(128)}, f32[2,8,128]{2,1,0:T(8,128)S(1)}, ...), condition=%wide.region_14.15_spmd.clone, body=%wide.region_10.14_spmd.clone.sunk | while | flops 551591552 | bytes 26622240 | solution.py:213
  610.6 1.0 constant_dynamic-slice_fusion.3
  611.7 2.8 fusion.133
  614.6 3.2 fusion.134
  617.9 3.9 fusion.136
  621.8 0.9 copy-done.5
  623.1 1.0 constant_dynamic-slice_fusion.3
  624.3 2.8 fusion.133
  627.1 3.2 fusion.134
  630.4 3.9 fusion.136
  634.3 0.9 copy-done.5
  635.3 1.7 fusion.70
  637.0 0.3 copy.61
  637.4 0.9 copy.81
  (152 shorter events, 3.2 us)
Async XLA Ops:
  7.2 82.7 %copy-start = (bf16[1024,1024]{1,0:T(8,128)(2,1)S(1)}, bf16[1024,1024]{1,0:T(8,128)(2,1)}, u32[]{:S(2)}) copy-start(bf16[1024,1024]{1,0:T(8,128)(2,1)} %param.22) | copy-start | bytes 6291460
  7.2 42.2 %all-gather.6.cloned.1.call-start = ((), (), s32[]{:S(2)}) async-start(), calls=%async_computation | async-start | bytes 4718592 | tf_op jit(solution)/shard_map/all_gather | solution.py:132
  7.9 342.8 %all-gather.8.cloned.1.call-start = ((), (), s32[]{:S(2)}) async-start(), calls=%async_computation.1 | async-start | bytes 20971520 | tf_op jit(solution)/shard_map/all_gather | solution.py:133
  49.4 1.9 copy-start.3
  49.4 2.3 copy-start.9
  49.4 337.5 %all-gather.10.cloned.1.call-start = ((), (), s32[]{:S(2)}) async-start(), calls=%async_computation.2 | async-start | bytes 4718592 | tf_op jit(solution)/shard_map/all_gather | solution.py:148
  50.1 376.0 %all-gather.14.cloned.1.call-start = ((), (), s32[]{:S(2)}) async-start(), calls=%async_computation.4 | async-start | bytes 4718592 | tf_op jit(solution)/shard_map/all_gather | solution.py:152
  50.7 538.0 %all-gather.12.cloned.1.call-start = ((), (), s32[]{:S(2)}) async-start(), calls=%async_computation.3 | async-start | bytes 37748736 | tf_op jit(solution)/shard_map/all_gather | solution.py:144
  51.7 13.1 %copy-start.11 = (s32[8]{0:T(128)S(1)}, s32[8]{0:T(128)}, u32[]{:S(2)}) copy-start(s32[8]{0:T(128)} %param.19) | copy-start | bytes 100
  51.7 13.9 %copy-start.8 = (bf16[31,1024]{1,0:T(8,128)(2,1)S(1)}, bf16[31,1024]{1,0:T(8,128)(2,1)}, u32[]{:S(2)}) copy-start(bf16[31,1024]{1,0:T(8,128)(2,1)} %param.25) | copy-start | bytes 190468
  56.3 13.0 %collective-permute-start.1 = (bf16[128,1024]{1,0:T(8,128)(2,1)S(1)}, bf16[128,1024]{1,0:T(8,128)(2,1)S(1)}, u32[]{:S(2)}, u32[]{:S(2)}) collective-permute-start(bf16[128,1024]{1,0:T(8,128)(2,1)S(1)} %get-tuple-element.316), channel_id=1, source_target_pairs={{0,1},{1,2},{2,3},{3,4},{4,5},{5,6},{6,7},{7,8},{8,9},{9,10},{10,1... | collective-permute-start | bytes 786440 | tf_op jit(solution)/shard_map/ppermute | solution.py:18
  59.7 20.3 %collective-permute-start = (bf16[128,1024]{1,0:T(8,128)(2,1)}, bf16[128,1024]{1,0:T(8,128)(2,1)}, u32[]{:S(2)}, u32[]{:S(2)}) collective-permute-start(bf16[128,1024]{1,0:T(8,128)(2,1)} %get-tuple-element.318), channel_id=1, source_target_pairs={{0,1},{1,2},{2,3},{3,4},{4,5},{5,6},{6,7},{7,8},{8,9},{9,10},{10,1... | collective-permute-start | bytes 786440 | tf_op jit(solution)/shard_map/ppermute | solution.py:18
  82.1 2.0 copy-start.6
  86.0 4.7 copy-start.44
  89.8 4.3 copy-start.45
  90.6 20.1 %copy-start.13 = (f32[1,1024]{1,0:T(1,128)S(1)}, f32[1,1024]{1,0:T(1,128)}, u32[]{:S(2)}) copy-start(f32[1,1024]{1,0:T(1,128)} %get-tuple-element.340) | copy-start | bytes 12292
  90.7 20.1 %copy-start.14 = (f32[1,1024]{1,0:T(1,128)S(1)}, f32[1,1024]{1,0:T(1,128)}, u32[]{:S(2)}) copy-start(f32[1,1024]{1,0:T(1,128)} %get-tuple-element.341) | copy-start | bytes 12292
  90.7 20.1 %copy-start.15 = (f32[1,1024]{1,0:T(1,128)S(1)}, f32[1,1024]{1,0:T(1,128)}, u32[]{:S(2)}) copy-start(f32[1,1024]{1,0:T(1,128)} %get-tuple-element.342) | copy-start | bytes 12292
  90.7 20.1 %copy-start.16 = (f32[1,1024]{1,0:T(1,128)S(1)}, f32[1,1024]{1,0:T(1,128)}, u32[]{:S(2)}) copy-start(f32[1,1024]{1,0:T(1,128)} %get-tuple-element.343) | copy-start | bytes 12292
  90.7 20.1 %copy-start.17 = (f32[1,1024]{1,0:T(1,128)S(1)}, f32[1,1024]{1,0:T(1,128)}, u32[]{:S(2)}) copy-start(f32[1,1024]{1,0:T(1,128)} %get-tuple-element.344) | copy-start | bytes 12292
  90.7 20.1 %copy-start.18 = (f32[1,1024]{1,0:T(1,128)S(1)}, f32[1,1024]{1,0:T(1,128)}, u32[]{:S(2)}) copy-start(f32[1,1024]{1,0:T(1,128)} %get-tuple-element.345) | copy-start | bytes 12292
  90.7 20.1 %copy-start.19 = (f32[1,1024]{1,0:T(1,128)S(1)}, f32[1,1024]{1,0:T(1,128)}, u32[]{:S(2)}) copy-start(f32[1,1024]{1,0:T(1,128)} %get-tuple-element.346) | copy-start | bytes 12292
  90.7 20.1 %copy-start.20 = (f32[1,1024]{1,0:T(1,128)S(1)}, f32[1,1024]{1,0:T(1,128)}, u32[]{:S(2)}) copy-start(f32[1,1024]{1,0:T(1,128)} %get-tuple-element.347) | copy-start | bytes 12292
  90.7 20.1 %copy-start.21 = (f32[1,1024]{1,0:T(1,128)S(1)}, f32[1,1024]{1,0:T(1,128)}, u32[]{:S(2)}) copy-start(f32[1,1024]{1,0:T(1,128)} %get-tuple-element.348) | copy-start | bytes 12292
  90.7 20.1 %copy-start.22 = (f32[1,1024]{1,0:T(1,128)S(1)}, f32[1,1024]{1,0:T(1,128)}, u32[]{:S(2)}) copy-start(f32[1,1024]{1,0:T(1,128)} %get-tuple-element.349) | copy-start | bytes 12292
  90.7 20.1 %copy-start.23 = (f32[1,1024]{1,0:T(1,128)S(1)}, f32[1,1024]{1,0:T(1,128)}, u32[]{:S(2)}) copy-start(f32[1,1024]{1,0:T(1,128)} %get-tuple-element.350) | copy-start | bytes 12292
  90.8 20.1 %copy-start.24 = (f32[1,1024]{1,0:T(1,128)S(1)}, f32[1,1024]{1,0:T(1,128)}, u32[]{:S(2)}) copy-start(f32[1,1024]{1,0:T(1,128)} %get-tuple-element.351) | copy-start | bytes 12292
  90.8 20.1 %copy-start.25 = (f32[1,1024]{1,0:T(1,128)S(1)}, f32[1,1024]{1,0:T(1,128)}, u32[]{:S(2)}) copy-start(f32[1,1024]{1,0:T(1,128)} %get-tuple-element.321) | copy-start | bytes 12292
  90.8 20.1 %copy-start.26 = (f32[1,1024]{1,0:T(1,128)S(1)}, f32[1,1024]{1,0:T(1,128)}, u32[]{:S(2)}) copy-start(f32[1,1024]{1,0:T(1,128)} %get-tuple-element.322) | copy-start | bytes 12292
  90.8 20.1 %copy-start.27 = (f32[1,1024]{1,0:T(1,128)S(1)}, f32[1,1024]{1,0:T(1,128)}, u32[]{:S(2)}) copy-start(f32[1,1024]{1,0:T(1,128)} %get-tuple-element.323) | copy-start | bytes 12292
  90.8 20.1 %copy-start.28 = (f32[1,1024]{1,0:T(1,128)S(1)}, f32[1,1024]{1,0:T(1,128)}, u32[]{:S(2)}) copy-start(f32[1,1024]{1,0:T(1,128)} %get-tuple-element.324) | copy-start | bytes 12292
  90.8 20.1 %copy-start.29 = (f32[1,1024]{1,0:T(1,128)S(1)}, f32[1,1024]{1,0:T(1,128)}, u32[]{:S(2)}) copy-start(f32[1,1024]{1,0:T(1,128)} %get-tuple-element.325) | copy-start | bytes 12292
  90.8 20.1 %copy-start.30 = (f32[1,1024]{1,0:T(1,128)S(1)}, f32[1,1024]{1,0:T(1,128)}, u32[]{:S(2)}) copy-start(f32[1,1024]{1,0:T(1,128)} %get-tuple-element.326) | copy-start | bytes 12292
  90.8 20.1 %copy-start.31 = (f32[1,1024]{1,0:T(1,128)S(1)}, f32[1,1024]{1,0:T(1,128)}, u32[]{:S(2)}) copy-start(f32[1,1024]{1,0:T(1,128)} %get-tuple-element.327) | copy-start | bytes 12292
  90.8 20.1 %copy-start.32 = (f32[1,1024]{1,0:T(1,128)S(1)}, f32[1,1024]{1,0:T(1,128)}, u32[]{:S(2)}) copy-start(f32[1,1024]{1,0:T(1,128)} %get-tuple-element.328) | copy-start | bytes 12292
  90.8 20.1 %copy-start.33 = (f32[1,1024]{1,0:T(1,128)S(1)}, f32[1,1024]{1,0:T(1,128)}, u32[]{:S(2)}) copy-start(f32[1,1024]{1,0:T(1,128)} %get-tuple-element.329) | copy-start | bytes 12292
  90.9 20.1 %copy-start.34 = (f32[1,1024]{1,0:T(1,128)S(1)}, f32[1,1024]{1,0:T(1,128)}, u32[]{:S(2)}) copy-start(f32[1,1024]{1,0:T(1,128)} %get-tuple-element.330) | copy-start | bytes 12292
  90.9 20.1 %copy-start.35 = (f32[1,1024]{1,0:T(1,128)S(1)}, f32[1,1024]{1,0:T(1,128)}, u32[]{:S(2)}) copy-start(f32[1,1024]{1,0:T(1,128)} %get-tuple-element.331) | copy-start | bytes 12292
  90.9 20.1 %copy-start.36 = (f32[1,1024]{1,0:T(1,128)S(1)}, f32[1,1024]{1,0:T(1,128)}, u32[]{:S(2)}) copy-start(f32[1,1024]{1,0:T(1,128)} %get-tuple-element.332) | copy-start | bytes 12292
  90.9 20.1 %copy-start.37 = (f32[1,1024]{1,0:T(1,128)S(1)}, f32[1,1024]{1,0:T(1,128)}, u32[]{:S(2)}) copy-start(f32[1,1024]{1,0:T(1,128)} %get-tuple-element.333) | copy-start | bytes 12292
  90.9 20.1 %copy-start.38 = (f32[1,1024]{1,0:T(1,128)S(1)}, f32[1,1024]{1,0:T(1,128)}, u32[]{:S(2)}) copy-start(f32[1,1024]{1,0:T(1,128)} %get-tuple-element.334) | copy-start | bytes 12292
  90.9 20.1 %copy-start.39 = (f32[1,1024]{1,0:T(1,128)S(1)}, f32[1,1024]{1,0:T(1,128)}, u32[]{:S(2)}) copy-start(f32[1,1024]{1,0:T(1,128)} %get-tuple-element.335) | copy-start | bytes 12292
  90.9 20.1 %copy-start.40 = (f32[1,1024]{1,0:T(1,128)S(1)}, f32[1,1024]{1,0:T(1,128)}, u32[]{:S(2)}) copy-start(f32[1,1024]{1,0:T(1,128)} %get-tuple-element.336) | copy-start | bytes 12292
  90.9 20.1 %copy-start.41 = (f32[1,1024]{1,0:T(1,128)S(1)}, f32[1,1024]{1,0:T(1,128)}, u32[]{:S(2)}) copy-start(f32[1,1024]{1,0:T(1,128)} %get-tuple-element.337) | copy-start | bytes 12292
  90.9 20.1 %copy-start.42 = (f32[1,1024]{1,0:T(1,128)S(1)}, f32[1,1024]{1,0:T(1,128)}, u32[]{:S(2)}) copy-start(f32[1,1024]{1,0:T(1,128)} %get-tuple-element.338) | copy-start | bytes 12292
  90.9 20.1 %copy-start.43 = (f32[1,1024]{1,0:T(1,128)S(1)}, f32[1,1024]{1,0:T(1,128)}, u32[]{:S(2)}) copy-start(f32[1,1024]{1,0:T(1,128)} %get-tuple-element.339) | copy-start | bytes 12292
  91.0 20.1 %copy-start.46 = (bf16[1024,1024]{1,0:T(8,128)(2,1)S(1)}, bf16[1024,1024]{1,0:T(8,128)(2,1)}, u32[]{:S(2)}) copy-start(bf16[1024,1024]{1,0:T(8,128)(2,1)} %param.26) | copy-start | bytes 6291460
  94.3 16.3 %collective-permute-start.2 = (bf16[30,1024]{1,0:T(8,128)(2,1)S(1)}, bf16[30,1024]{1,0:T(8,128)(2,1)S(1)}, u32[]{:S(2)}, u32[]{:S(2)}) collective-permute-start(bf16[30,1024]{1,0:T(8,128)(2,1)S(1)} %slice.294), channel_id=1, source_target_pairs={{0,1},{1,2},{2,3},{3,4},{4,5},{5,6},{6,7},{7,8},{8,9},{9,10},{10,1... | collective-permute-start | bytes 184328 | tf_op jit(solution)/shard_map/ppermute | solution.py:18
  113.6 245.4 %copy-start.7 = (bf16[128,1024]{1,0:T(8,128)(2,1)}, bf16[128,1024]{1,0:T(8,128)(2,1)S(1)}, u32[]{:S(2)}) copy-start(bf16[128,1024]{1,0:T(8,128)(2,1)S(1)} %fusion.23) | copy-start | bytes 786436
  150.6 208.4 %copy-start.10 = (f32[8192]{0:T(1024)S(1)}, f32[8192]{0:T(1024)}, u32[]{:S(2)}) copy-start(f32[8192]{0:T(1024)} %param.28) | copy-start | bytes 98308
  603.0 7.2 %copy-start.2 = (bf16[1024,256]{1,0:T(8,128)(2,1)S(1)}, bf16[1024,256]{1,0:T(8,128)(2,1)}, u32[]{:S(2)}) copy-start(bf16[1024,256]{1,0:T(8,128)(2,1)} %all_gather.28) | copy-start | bytes 1572868
  603.0 7.2 %copy-start.12 = (s32[8]{0:T(128)S(1)}, s32[8]{0:T(128)}, u32[]{:S(2)}) copy-start(s32[8]{0:T(128)} %param.19) | copy-start | bytes 100
  611.7 6.2 copy-start.4
  621.8 1.0 copy-start.5
  624.2 6.2 copy-start.4
  634.3 1.0 copy-start.5
  635.3 3.0 copy-start.1
Sparse Core Ops, SparseCore 0:
  9.9 39.4 all-gather.5
  50.9 299.7 all-gather.7
  352.7 34.2 all-gather.9
  388.7 37.3 all-gather.13
  427.8 160.7 all-gather.11
where the time goes:
time: 646 us; the launch traced here: 645 us
  waiting for transfers between devices  458 us (71%)
  blocking collectives  59.4 us (9%)
  matrix products  58.1 us (9%)
  starting transfers between devices  20.9 us (3%)
  other arithmetic  18.1 us (3%)
  local copies, waits for them, and re-layouts  15.7 us (2%)
  between operations  14.7 us (2%)
    all_gather x1, waiting for transfers between devices, on_device(): adapter_full = lax.all_gather(adapter_part, 'mp', axis=1, tiled=True)  200 us
    all_gather x1, waiting for transfers between devices, on_device(): lax.all_gather(w_query, 'tm', axis=0, tiled=True)  149 us
    all_gather x1, waiting for transfers between devices, on_device(): adapter_part = lax.all_gather(w_adapter, 'tm', axis=0, tiled=True)  41.4 us
    all_gather x1, blocking collectives, on_device(): shard_pooled = lax.all_gather(pooled, 'mp', axis=0, tiled=True)  36.5 us
    all_gather x1, waiting for transfers between devices, on_device(): lax.all_gather(w_key, 'tm', axis=0, tiled=True)  27.4 us
    all_gather x1, waiting for transfers between devices, on_device(): lax.all_gather(w_value, 'tm', axis=0, tiled=True)  23.5 us
    ppermute x3, starting transfers between devices, passed_along(): return lax.ppermute(value, axis, pairs)  20.7 us
    ppermute x3, waiting for transfers between devices, passed_along(): return lax.ppermute(value, axis, pairs)  14.1 us
  transfers between devices with their start and end apart: 8, of which 8 were waited for; matrix products, arithmetic and copies ran while one was open for 7% of the time, Pallas kernels for 0%

commit v1 on v0

--- a/solution.py
+++ b/solution.py
@@ -10,6 +10,23 @@
 eps_llm = 1e-06
 rope_base = 1000000.0
 masked_score = -1e30
+
+
+def joined_along(blocks, dim):
+    dims = list(blocks.shape[1:])
+    dims[dim] *= blocks.shape[0]
+    return jnp.moveaxis(blocks, 0, dim).reshape(dims)
+
+
+def grow_blocks(shard, axis):
+    count, index = (lax.axis_size(axis), lax.axis_index(axis))
+    blocks, apart = (shard[None], 1)
+    while apart < count:
+        other = lax.ppermute(blocks, axis, [(i, i ^ apart) for i in range(count)])
+        low = index & apart == 0
+        blocks = jnp.concatenate([jnp.where(low, blocks, other), jnp.where(low, other, blocks)])
+        apart *= 2
+    return blocks
 
 
 def passed_along(value, axis, by):
@@ -129,7 +146,7 @@
     ).astype(jnp.bfloat16)
     shard_pooled = lax.all_gather(pooled, "mp", axis=0, tiled=True)
     shard_tokens = shard_pooled.shape[0]
-    adapter_part = lax.all_gather(w_adapter, "tm", axis=0, tiled=True)
+    adapter_part = joined_along(grow_blocks(w_adapter, "tm"), 0)
     adapter_full = lax.all_gather(adapter_part, "mp", axis=1, tiled=True)
     adapted = jnp.dot(shard_pooled, adapter_full, preferred_element_type=jnp.float32)
     llm_in = (

time: 646 us -> 690 us (1.068)
  waiting for transfers between devices: 458 us -> 486 us
  other arithmetic: 18.1 us -> 26.9 us
    ppermute x0 -> x3, waiting for transfers between devices: none -> 71 us  [grow_blocks(): other = lax.ppermute(blocks, axis, [(i, i ^ apart) for i in range(count)])]
    all_gather x1 -> x0, waiting for transfers between devices: 41.4 us -> none  [on_device(): adapter_part = lax.all_gather(w_adapter, 'tm', axis=0, tiled=True)]
  transfers between devices with their start and end apart: 8 -> 10, of which waited for: 8 -> 10; matrix products, arithmetic and copies ran while one was open for 7% -> 6% of each run, Pallas kernels for 0% -> 0%
where the time goes in v1:
time: 690 us; the launch traced here: 689 us
  waiting for transfers between devices  486 us (70%)
  blocking collectives  60.1 us (9%)
  matrix products  58.1 us (8%)
  other arithmetic  26.9 us (4%)
  starting transfers between devices  26.3 us (4%)
  local copies, waits for them, and re-layouts  17.6 us (3%)
  between operations  14.7 us (2%)
    all_gather x1, waiting for transfers between devices, on_device(): adapter_full = lax.all_gather(adapter_part, 'mp', axis=1, tiled=True)  201 us
    all_gather x1, waiting for transfers between devices, on_device(): lax.all_gather(w_query, 'tm', axis=0, tiled=True)  149 us
    ppermute x3, waiting for transfers between devices, grow_blocks(): other = lax.ppermute(blocks, axis, [(i, i ^ apart) for i in range(count)])  71 us
    all_gather x1, blocking collectives, on_device(): shard_pooled = lax.all_gather(pooled, 'mp', axis=0, tiled=True)  37.3 us
    all_gather x1, waiting for transfers between devices, on_device(): lax.all_gather(w_key, 'tm', axis=0, tiled=True)  27.1 us
    all_gather x1, waiting for transfers between devices, on_device(): lax.all_gather(w_value, 'tm', axis=0, tiled=True)  23.7 us
    ppermute x3, starting transfers between devices, passed_along(): return lax.ppermute(value, axis, pairs)  21 us
  transfers between devices with their start and end apart: 10, of which 10 were waited for; matrix products, arithmetic and copies ran while one was open for 6% of the time, Pallas kernels for 0%

profile of v1, /device:TPU:0, one launch (start us, length us, event | category | flops | bytes accessed | tf_op | source)
XLA Modules:
  0.0 689.5 jit_solution(9937296401977920123)
XLA Ops:
  7.7 1.7 collective-permute-done.3
  9.5 1.1 broadcast_select_fusion.5
  10.6 0.8 copy-done.5
  11.6 2.9 collective-permute-start.4
  14.4 23.6 %collective-permute-done.4 = bf16[2,128,2048]{2,1,0:T(8,128)(2,1)} collective-permute-done((bf16[2,128,2048]{2,1,0:T(8,128)(2,1)S(1)}, bf16[2,128,2048]{2,1,0:T(8,128)(2,1)}, u32[]{:S(2)}, u32[]{:S(2)}) %collective-permute-start.4) | collective-permute-done | bytes 1048608 | tf_op jit(solution)/shard_map/ppermute | solution.py:25
  38.0 1.7 broadcast_select_fusion.3
  39.7 1.0 copy-done.2
  40.7 1.5 pad_maximum_fusion.1
  42.2 1.8 collective-permute-start.5
  44.0 45.7 %collective-permute-done.5 = bf16[4,128,2048]{2,1,0:T(8,128)(2,1)} collective-permute-done((bf16[4,128,2048]{2,1,0:T(8,128)(2,1)}, bf16[4,128,2048]{2,1,0:T(8,128)(2,1)}, u32[]{:S(2)}, u32[]{:S(2)}) %collective-permute-start.5) | collective-permute-done | bytes 2097184 | tf_op jit(solution)/shard_map/ppermute | solution.py:25
  89.7 2.1 broadcast_select_fusion.1
  91.8 2.4 pad_maximum_fusion
  94.2 0.7 all-gather.7.cloned.1.call-update
  95.0 0.7 all-gather.11.cloned.1.call-update
  95.7 0.5 all-gather.9.cloned.1.call-update
  96.6 3.9 convolution_convert_fusion
  100.5 0.8 fusion.92
  101.3 3.4 collective-permute-start.1
  104.7 4.2 collective-permute-start
  109.0 0.9 broadcast_add_fusion
  109.9 0.7 or_and_fusion.1
  110.7 0.7 fusion.94
  111.3 0.7 fusion.93
  112.4 0.8 copy.53
  113.3 0.6 subtract_compare_fusion.1
  114.4 8.9 %collective-permute-done = bf16[128,1024]{1,0:T(8,128)(2,1)} collective-permute-done((bf16[128,1024]{1,0:T(8,128)(2,1)}, bf16[128,1024]{1,0:T(8,128)(2,1)}, u32[]{:S(2)}, u32[]{:S(2)}) %collective-permute-start) | collective-permute-done | bytes 262176 | tf_op jit(solution)/shard_map/ppermute | solution.py:35
  123.3 1.1 pad_maximum_fusion.3
  124.4 1.0 copy.52
  125.4 2.0 fusion.95
  127.4 1.9 fusion.97
  129.3 3.8 fusion.22
  133.1 0.5 fusion.96
  134.2 3.2 fusion.72
  137.6 13.4 %collective-permute-start.2 = (bf16[30,1024]{1,0:T(8,128)(2,1)S(1)}, bf16[30,1024]{1,0:T(8,128)(2,1)S(1)}, u32[]{:S(2)}, u32[]{:S(2)}) collective-permute-start(bf16[30,1024]{1,0:T(8,128)(2,1)S(1)} %slice.294), channel_id=1, source_target_pairs={{0,1},{1,2},{2,3},{3,4},{4,5},{5,6},{6,7},{7,8},{8,9},{9,10},{10,1... | collective-permute-start | bytes 184328 | tf_op jit(solution)/shard_map/ppermute | solution.py:35
  151.1 3.0 collective-permute-done.2
  154.5 2.5 fusion.23
  157.5 37.3 %all_gather.21 = bf16[128,1024]{1,0:T(8,128)(2,1)S(1)} all-gather(bf16[32,1024]{1,0:T(8,128)(2,1)S(1)} %multiply_convert_fusion.5), channel_id=1, replica_groups=mesh['tm'=8,'mp'=4] {'mp'}, dimensions={0}, use_global_device_ids=true | all-gather | bytes 327680 | tf_op jit(solution)/shard_map/all_gather | solution.py:147
  194.8 200.7 %all-gather.5.cloned.1.call-done = bf16[1024,8192]{1,0:T(8,128)(2,1)} async-done(((bf16[1024,2048]{1,0:T(8,128)(2,1)}), bf16[1024,8192]{1,0:T(8,128)(2,1)}) %all-gather.5.cloned.1.call-update) | async-done | bytes 16777232 | tf_op jit(solution)/shard_map/all_gather | solution.py:150
  395.6 8.3 %multiply_reduce_fusion = (f32[128]{0:T(128)S(1)}, f32[128,8192]{1,0:T(8,128)S(1)}) fusion(bf16[128,1024]{1,0:T(8,128)(2,1)S(1)} %all_gather.21, bf16[1024,8192]{1,0:T(8,128)(2,1)} %all-gather.5.cloned.1.call-done), kind=kOutput, calls=%fused_computation.36 | convolution fusion | flops 2149580800 | bytes 21234176 | tf_op jit(solution)/shard_map/dot_general | solution.py:151
  404.4 27.1 %all-gather.7.cloned.1.call-done = bf16[8192,256]{1,0:T(8,128)(2,1)} async-done(((bf16[1024,256]{1,0:T(8,128)(2,1)}), bf16[8192,256]{1,0:T(8,128)(2,1)}) %all-gather.7.cloned.1.call-update) | async-done | bytes 4194320 | tf_op jit(solution)/shard_map/all_gather | solution.py:165
  431.5 2.9 fusion.98
  435.0 12.0 %all_gather.24 = bf16[1024,256]{1,0:T(8,128)(2,1)} all-gather(bf16[128,256]{1,0:T(8,128)(2,1)S(1)} %fusion.82), channel_id=1, replica_groups=mesh['tm'=8,'mp'=4] {'tm'}, dimensions={0}, use_global_device_ids=true | all-gather | bytes 589824 | tf_op jit(solution)/shard_map/all_gather | solution.py:193
  447.0 23.7 %all-gather.11.cloned.1.call-done = bf16[8192,256]{1,0:T(8,128)(2,1)} async-done(((bf16[1024,256]{1,0:T(8,128)(2,1)}), bf16[8192,256]{1,0:T(8,128)(2,1)}) %all-gather.11.cloned.1.call-update) | async-done | bytes 4194320 | tf_op jit(solution)/shard_map/all_gather | solution.py:169
  470.7 2.9 convolution_convert_fusion.1
  473.6 10.8 %all_gather.27 = bf16[1024,256]{1,0:T(8,128)(2,1)} all-gather(bf16[128,256]{1,0:T(8,128)(2,1)S(1)} %convolution_convert_fusion.1), channel_id=1, replica_groups=mesh['tm'=8,'mp'=4] {'tm'}, dimensions={0}, use_global_device_ids=true | all-gather | bytes 589824 | tf_op jit(solution)/shard_map/all_gather | solution.py:194
  484.4 148.9 %all-gather.9.cloned.1.call-done = bf16[8192,2048]{1,0:T(8,128)(2,1)} async-done(((bf16[1024,2048]{1,0:T(8,128)(2,1)}), bf16[8192,2048]{1,0:T(8,128)(2,1)}) %all-gather.9.cloned.1.call-update) | async-done | bytes 33554448 | tf_op jit(solution)/shard_map/all_gather | solution.py:161
  633.3 12.9 %fusion.99 = f32[128,2048]{1,0:T(8,128)S(1)} fusion(bf16[128,8192]{1,0:T(8,128)(2,1)S(1)} %multiply_convert_fusion, bf16[8192,2048]{1,0:T(8,128)(2,1)} %all-gather.9.cloned.1.call-done), kind=kOutput, calls=%fused_computation.208 | convolution fusion | flops 4294967296 | bytes 36700160 | tf_op jit(solution)/shard_map/dot_general | solution.py:159
  646.5 1.1 slice_negate_fusion
  647.6 2.4 copy.57
  650.0 2.4 copy.58
  652.6 2.2 fusion.25
  654.8 25.1 %while.20 = (s32[]{:T(128)}, f32[2,8,128]{2,1,0:T(8,128)S(1)}, f32[2,8,128]{2,1,0:T(8,128)S(1)}, f32[2,8,128,128]{3,2,1,0:T(8,128)}, s32[8]{0:T(128)S(1)}, /*ind...) while((s32[]{:T(128)}, f32[2,8,128]{2,1,0:T(8,128)S(1)}, ...), condition=%wide.region_14.15_spmd.clone, body=%wide.region_10.14_spmd.clone.sunk | while | flops 551591552 | bytes 26622240 | solution.py:230
  655.2 1.0 constant_dynamic-slice_fusion.3
  656.4 2.8 fusion.133
  659.2 3.2 fusion.134
  662.5 3.9 fusion.136
  666.4 1.0 copy-done.8
  667.7 1.0 constant_dynamic-slice_fusion.3
  668.9 2.8 fusion.133
  671.7 3.2 fusion.134
  675.0 3.9 fusion.136
  678.9 1.0 copy-done.8
  679.9 1.7 fusion.70
  682.0 0.9 copy.81
  (167 shorter events, 6.8 us)
Async XLA Ops:
  7.2 125.9 %copy-start = (bf16[1024,1024]{1,0:T(8,128)(2,1)S(1)}, bf16[1024,1024]{1,0:T(8,128)(2,1)}, u32[]{:S(2)}) copy-start(bf16[1024,1024]{1,0:T(8,128)(2,1)} %param.22) | copy-start | bytes 6291460
  7.2 388.4 %all-gather.5.cloned.1.call-start = ((), (), s32[]{:S(2)}) async-start(), calls=%async_computation | async-start | bytes 20971520 | tf_op jit(solution)/shard_map/all_gather | solution.py:150
  7.2 2.3 collective-permute-start.3
  10.6 0.8 copy-start.5
  10.6 1.0 copy-start.6
  11.6 26.4 %collective-permute-start.4 = (bf16[2,128,2048]{2,1,0:T(8,128)(2,1)S(1)}, bf16[2,128,2048]{2,1,0:T(8,128)(2,1)}, u32[]{:S(2)}, u32[]{:S(2)}) collective-permute-start(bf16[2,128,2048]{2,1,0:T(8,128)(2,1)S(1)} %pad_maximum_fusion.2), channel_id=1, source_target_pairs={{0,8},{4,12},{8,0},{12,4},{16,24},{20,28},{24,16},{28,20},{1,9},{5... | collective-permute-start | bytes 3145736 | tf_op jit(solution)/shard_map/ppermute | solution.py:25
  39.7 1.0 copy-start.2
  42.2 47.5 %collective-permute-start.5 = (bf16[4,128,2048]{2,1,0:T(8,128)(2,1)}, bf16[4,128,2048]{2,1,0:T(8,128)(2,1)}, u32[]{:S(2)}, u32[]{:S(2)}) collective-permute-start(bf16[4,128,2048]{2,1,0:T(8,128)(2,1)} %pad_maximum_fusion.1), channel_id=1, source_target_pairs={{0,16},{4,20},{8,24},{12,28},{16,0},{20,4},{24,8},{28,12},{1,17},{... | collective-permute-start | bytes 6291464 | tf_op jit(solution)/shard_map/ppermute | solution.py:25
  94.1 2.1 copy-start.4
  94.1 2.5 copy-start.12
  94.2 337.3 %all-gather.7.cloned.1.call-start = ((), (), s32[]{:S(2)}) async-start(), calls=%async_computation.1 | async-start | bytes 4718592 | tf_op jit(solution)/shard_map/all_gather | solution.py:165
  94.9 375.8 %all-gather.11.cloned.1.call-start = ((), (), s32[]{:S(2)}) async-start(), calls=%async_computation.3 | async-start | bytes 4718592 | tf_op jit(solution)/shard_map/all_gather | solution.py:169
  95.7 537.6 %all-gather.9.cloned.1.call-start = ((), (), s32[]{:S(2)}) async-start(), calls=%async_computation.2 | async-start | bytes 37748736 | tf_op jit(solution)/shard_map/all_gather | solution.py:161
  96.6 13.2 %copy-start.14 = (s32[8]{0:T(128)S(1)}, s32[8]{0:T(128)}, u32[]{:S(2)}) copy-start(s32[8]{0:T(128)} %param.19) | copy-start | bytes 100
  96.6 14.0 %copy-start.11 = (bf16[31,1024]{1,0:T(8,128)(2,1)S(1)}, bf16[31,1024]{1,0:T(8,128)(2,1)}, u32[]{:S(2)}) copy-start(bf16[31,1024]{1,0:T(8,128)(2,1)} %param.25) | copy-start | bytes 190468
  101.3 12.9 %collective-permute-start.1 = (bf16[128,1024]{1,0:T(8,128)(2,1)S(1)}, bf16[128,1024]{1,0:T(8,128)(2,1)S(1)}, u32[]{:S(2)}, u32[]{:S(2)}) collective-permute-start(bf16[128,1024]{1,0:T(8,128)(2,1)S(1)} %get-tuple-element.322), channel_id=1, source_target_pairs={{0,1},{1,2},{2,3},{3,4},{4,5},{5,6},{6,7},{7,8},{8,9},{9,10},{10,1... | collective-permute-start | bytes 786440 | tf_op jit(solution)/shard_map/ppermute | solution.py:35
  104.7 18.6 %collective-permute-start = (bf16[128,1024]{1,0:T(8,128)(2,1)}, bf16[128,1024]{1,0:T(8,128)(2,1)}, u32[]{:S(2)}, u32[]{:S(2)}) collective-permute-start(bf16[128,1024]{1,0:T(8,128)(2,1)} %get-tuple-element.324), channel_id=1, source_target_pairs={{0,1},{1,2},{2,3},{3,4},{4,5},{5,6},{6,7},{7,8},{8,9},{9,10},{10,1... | collective-permute-start | bytes 786440 | tf_op jit(solution)/shard_map/ppermute | solution.py:35
  125.4 2.0 copy-start.9
  129.3 4.6 copy-start.47
  133.1 4.3 copy-start.48
  133.9 20.3 %copy-start.16 = (f32[1,1024]{1,0:T(1,128)S(1)}, f32[1,1024]{1,0:T(1,128)}, u32[]{:S(2)}) copy-start(f32[1,1024]{1,0:T(1,128)} %get-tuple-element.346) | copy-start | bytes 12292
  133.9 20.3 %copy-start.17 = (f32[1,1024]{1,0:T(1,128)S(1)}, f32[1,1024]{1,0:T(1,128)}, u32[]{:S(2)}) copy-start(f32[1,1024]{1,0:T(1,128)} %get-tuple-element.347) | copy-start | bytes 12292
  133.9 20.3 %copy-start.18 = (f32[1,1024]{1,0:T(1,128)S(1)}, f32[1,1024]{1,0:T(1,128)}, u32[]{:S(2)}) copy-start(f32[1,1024]{1,0:T(1,128)} %get-tuple-element.348) | copy-start | bytes 12292
  133.9 20.3 %copy-start.19 = (f32[1,1024]{1,0:T(1,128)S(1)}, f32[1,1024]{1,0:T(1,128)}, u32[]{:S(2)}) copy-start(f32[1,1024]{1,0:T(1,128)} %get-tuple-element.349) | copy-start | bytes 12292
  133.9 20.3 %copy-start.20 = (f32[1,1024]{1,0:T(1,128)S(1)}, f32[1,1024]{1,0:T(1,128)}, u32[]{:S(2)}) copy-start(f32[1,1024]{1,0:T(1,128)} %get-tuple-element.350) | copy-start | bytes 12292
  133.9 20.3 %copy-start.21 = (f32[1,1024]{1,0:T(1,128)S(1)}, f32[1,1024]{1,0:T(1,128)}, u32[]{:S(2)}) copy-start(f32[1,1024]{1,0:T(1,128)} %get-tuple-element.351) | copy-start | bytes 12292
  134.0 20.3 %copy-start.22 = (f32[1,1024]{1,0:T(1,128)S(1)}, f32[1,1024]{1,0:T(1,128)}, u32[]{:S(2)}) copy-start(f32[1,1024]{1,0:T(1,128)} %get-tuple-element.352) | copy-start | bytes 12292
  134.0 20.3 %copy-start.23 = (f32[1,1024]{1,0:T(1,128)S(1)}, f32[1,1024]{1,0:T(1,128)}, u32[]{:S(2)}) copy-start(f32[1,1024]{1,0:T(1,128)} %get-tuple-element.353) | copy-start | bytes 12292
  134.0 20.3 %copy-start.24 = (f32[1,1024]{1,0:T(1,128)S(1)}, f32[1,1024]{1,0:T(1,128)}, u32[]{:S(2)}) copy-start(f32[1,1024]{1,0:T(1,128)} %get-tuple-element.354) | copy-start | bytes 12292
  134.0 20.3 %copy-start.25 = (f32[1,1024]{1,0:T(1,128)S(1)}, f32[1,1024]{1,0:T(1,128)}, u32[]{:S(2)}) copy-start(f32[1,1024]{1,0:T(1,128)} %get-tuple-element.355) | copy-start | bytes 12292
  134.0 20.3 %copy-start.26 = (f32[1,1024]{1,0:T(1,128)S(1)}, f32[1,1024]{1,0:T(1,128)}, u32[]{:S(2)}) copy-start(f32[1,1024]{1,0:T(1,128)} %get-tuple-element.356) | copy-start | bytes 12292
  134.0 20.3 %copy-start.27 = (f32[1,1024]{1,0:T(1,128)S(1)}, f32[1,1024]{1,0:T(1,128)}, u32[]{:S(2)}) copy-start(f32[1,1024]{1,0:T(1,128)} %get-tuple-element.357) | copy-start | bytes 12292
  134.0 20.3 %copy-start.28 = (f32[1,1024]{1,0:T(1,128)S(1)}, f32[1,1024]{1,0:T(1,128)}, u32[]{:S(2)}) copy-start(f32[1,1024]{1,0:T(1,128)} %get-tuple-element.327) | copy-start | bytes 12292
  134.0 20.3 %copy-start.29 = (f32[1,1024]{1,0:T(1,128)S(1)}, f32[1,1024]{1,0:T(1,128)}, u32[]{:S(2)}) copy-start(f32[1,1024]{1,0:T(1,128)} %get-tuple-element.328) | copy-start | bytes 12292
  134.0 20.3 %copy-start.30 = (f32[1,1024]{1,0:T(1,128)S(1)}, f32[1,1024]{1,0:T(1,128)}, u32[]{:S(2)}) copy-start(f32[1,1024]{1,0:T(1,128)} %get-tuple-element.329) | copy-start | bytes 12292
  134.0 20.3 %copy-start.31 = (f32[1,1024]{1,0:T(1,128)S(1)}, f32[1,1024]{1,0:T(1,128)}, u32[]{:S(2)}) copy-start(f32[1,1024]{1,0:T(1,128)} %get-tuple-element.330) | copy-start | bytes 12292
  134.1 20.3 %copy-start.32 = (f32[1,1024]{1,0:T(1,128)S(1)}, f32[1,1024]{1,0:T(1,128)}, u32[]{:S(2)}) copy-start(f32[1,1024]{1,0:T(1,128)} %get-tuple-element.331) | copy-start | bytes 12292
  134.1 20.3 %copy-start.33 = (f32[1,1024]{1,0:T(1,128)S(1)}, f32[1,1024]{1,0:T(1,128)}, u32[]{:S(2)}) copy-start(f32[1,1024]{1,0:T(1,128)} %get-tuple-element.332) | copy-start | bytes 12292
  134.1 20.3 %copy-start.34 = (f32[1,1024]{1,0:T(1,128)S(1)}, f32[1,1024]{1,0:T(1,128)}, u32[]{:S(2)}) copy-start(f32[1,1024]{1,0:T(1,128)} %get-tuple-element.333) | copy-start | bytes 12292
  134.1 20.3 %copy-start.35 = (f32[1,1024]{1,0:T(1,128)S(1)}, f32[1,1024]{1,0:T(1,128)}, u32[]{:S(2)}) copy-start(f32[1,1024]{1,0:T(1,128)} %get-tuple-element.334) | copy-start | bytes 12292
  134.1 20.3 %copy-start.36 = (f32[1,1024]{1,0:T(1,128)S(1)}, f32[1,1024]{1,0:T(1,128)}, u32[]{:S(2)}) copy-start(f32[1,1024]{1,0:T(1,128)} %get-tuple-element.335) | copy-start | bytes 12292
  134.1 20.3 %copy-start.37 = (f32[1,1024]{1,0:T(1,128)S(1)}, f32[1,1024]{1,0:T(1,128)}, u32[]{:S(2)}) copy-start(f32[1,1024]{1,0:T(1,128)} %get-tuple-element.336) | copy-start | bytes 12292
  134.1 20.3 %copy-start.38 = (f32[1,1024]{1,0:T(1,128)S(1)}, f32[1,1024]{1,0:T(1,128)}, u32[]{:S(2)}) copy-start(f32[1,1024]{1,0:T(1,128)} %get-tuple-element.337) | copy-start | bytes 12292
  134.1 20.3 %copy-start.39 = (f32[1,1024]{1,0:T(1,128)S(1)}, f32[1,1024]{1,0:T(1,128)}, u32[]{:S(2)}) copy-start(f32[1,1024]{1,0:T(1,128)} %get-tuple-element.338) | copy-start | bytes 12292
  134.1 20.3 %copy-start.40 = (f32[1,1024]{1,0:T(1,128)S(1)}, f32[1,1024]{1,0:T(1,128)}, u32[]{:S(2)}) copy-start(f32[1,1024]{1,0:T(1,128)} %get-tuple-element.339) | copy-start | bytes 12292
  134.1 20.3 %copy-start.41 = (f32[1,1024]{1,0:T(1,128)S(1)}, f32[1,1024]{1,0:T(1,128)}, u32[]{:S(2)}) copy-start(f32[1,1024]{1,0:T(1,128)} %get-tuple-element.340) | copy-start | bytes 12292
  134.2 20.3 %copy-start.42 = (f32[1,1024]{1,0:T(1,128)S(1)}, f32[1,1024]{1,0:T(1,128)}, u32[]{:S(2)}) copy-start(f32[1,1024]{1,0:T(1,128)} %get-tuple-element.341) | copy-start | bytes 12292
  134.2 20.3 %copy-start.43 = (f32[1,1024]{1,0:T(1,128)S(1)}, f32[1,1024]{1,0:T(1,128)}, u32[]{:S(2)}) copy-start(f32[1,1024]{1,0:T(1,128)} %get-tuple-element.342) | copy-start | bytes 12292
  134.2 20.3 %copy-start.44 = (f32[1,1024]{1,0:T(1,128)S(1)}, f32[1,1024]{1,0:T(1,128)}, u32[]{:S(2)}) copy-start(f32[1,1024]{1,0:T(1,128)} %get-tuple-element.343) | copy-start | bytes 12292
  134.2 20.3 %copy-start.45 = (f32[1,1024]{1,0:T(1,128)S(1)}, f32[1,1024]{1,0:T(1,128)}, u32[]{:S(2)}) copy-start(f32[1,1024]{1,0:T(1,128)} %get-tuple-element.344) | copy-start | bytes 12292
  134.2 20.3 %copy-start.46 = (f32[1,1024]{1,0:T(1,128)S(1)}, f32[1,1024]{1,0:T(1,128)}, u32[]{:S(2)}) copy-start(f32[1,1024]{1,0:T(1,128)} %get-tuple-element.345) | copy-start | bytes 12292
  134.2 20.3 %copy-start.49 = (bf16[1024,1024]{1,0:T(8,128)(2,1)S(1)}, bf16[1024,1024]{1,0:T(8,128)(2,1)}, u32[]{:S(2)}) copy-start(bf16[1024,1024]{1,0:T(8,128)(2,1)} %param.26) | copy-start | bytes 6291460
  137.6 16.5 %collective-permute-start.2 = (bf16[30,1024]{1,0:T(8,128)(2,1)S(1)}, bf16[30,1024]{1,0:T(8,128)(2,1)S(1)}, u32[]{:S(2)}, u32[]{:S(2)}) collective-permute-start(bf16[30,1024]{1,0:T(8,128)(2,1)S(1)} %slice.294), channel_id=1, source_target_pairs={{0,1},{1,2},{2,3},{3,4},{4,5},{5,6},{6,7},{7,8},{8,9},{9,10},{10,1... | collective-permute-start | bytes 184328 | tf_op jit(solution)/shard_map/ppermute | solution.py:35
  157.0 246.8 %copy-start.10 = (bf16[128,1024]{1,0:T(8,128)(2,1)}, bf16[128,1024]{1,0:T(8,128)(2,1)S(1)}, u32[]{:S(2)}) copy-start(bf16[128,1024]{1,0:T(8,128)(2,1)S(1)} %fusion.23) | copy-start | bytes 786436
  194.8 209.0 %copy-start.13 = (f32[8192]{0:T(1024)S(1)}, f32[8192]{0:T(1024)}, u32[]{:S(2)}) copy-start(f32[8192]{0:T(1024)} %param.28) | copy-start | bytes 98308
  647.6 7.3 %copy-start.3 = (bf16[1024,256]{1,0:T(8,128)(2,1)S(1)}, bf16[1024,256]{1,0:T(8,128)(2,1)}, u32[]{:S(2)}) copy-start(bf16[1024,256]{1,0:T(8,128)(2,1)} %all_gather.24) | copy-start | bytes 1572868
  647.6 7.3 %copy-start.15 = (s32[8]{0:T(128)S(1)}, s32[8]{0:T(128)}, u32[]{:S(2)}) copy-start(s32[8]{0:T(128)} %param.19) | copy-start | bytes 100
  656.4 6.2 copy-start.7
  666.4 1.0 copy-start.8
  668.9 6.2 copy-start.7
  678.9 1.0 copy-start.8
  679.9 3.0 copy-start.1
Sparse Core Ops, SparseCore 0:
  94.3 301.2 all-gather.4
  397.5 33.9 all-gather.6
  433.4 37.2 all-gather.10
  472.4 160.7 all-gather.8
